TPU v7x, 128 devices: a whole 4x4x4 slice. The times are simulated.
128 devices in a mesh: hi: 16 (over y, x), lo: 8 (over z, core).
Axes of the slice: x: 4, y: 4, z: 4, core: 2. Of those that a mesh axis runs over, the one named last changes fastest.
Arguments:
- previous: float32 [32, 2097152], P(None, ('hi', 'lo')), may hold values from -6 to 6
- current: float32 [32, 2097152], P(None, ('hi', 'lo')), may hold values from -6 to 6
- field_levels: int32 [21], replicated, may hold values from -4 to 4
- bond_levels: int32 [20], replicated, may hold values from 1 to 3
Outputs:
- ortho_block: float32 [32, 2097152], P(None, ('hi', 'lo'))
- upper_factor: float32 [32, 32], replicated
All inputs are finite; a program needn't handle non-finite values.
Results may differ from a plain program's by a relative error of at most 0.00005.
Values sent between devices are 32-bit elements; how exact they have to be, the bound alone decides.
A program may use at most 64 MiB of HBM per device.

v0:
```python
import jax
import jax.numpy as jnp
from jax import lax
from jax.sharding import PartitionSpec as P

FIELD_STEP = 0.75
COUPLING_STEP = 0.5


def chain_matrix(couplings, bit_count, bond_list):
    width = 2**bit_count
    rows = lax.iota(jnp.int32, width)[:, None]
    cols = lax.iota(jnp.int32, width)[None, :]
    matrix = jnp.zeros((width, width), jnp.float32)
    for site_number, spot in bond_list:
        differ = cols >> spot & 1 != cols >> spot + 1 & 1
        target = rows == cols ^ 3 << spot
        matrix = matrix + jnp.where(differ & target, 0.5 * couplings[site_number], 0.0)
    return matrix


def cross_flip(values, coupling, low_spot):
    width = values.shape[-1]
    index = lax.iota(jnp.int32, width)
    permute = (index[:, None] == index[None, :] ^ 1 << low_spot).astype(jnp.float32)
    moved = jnp.einsum("vatbl,lj->vatbj", values, permute, precision=lax.Precision.HIGHEST)
    flipped = jnp.flip(moved, axis=2)
    upper = lax.iota(jnp.int32, 2)[:, None]
    keep = (index[None, :] >> low_spot & 1 != upper).astype(jnp.float32)
    return 0.5 * coupling * flipped * keep[None, None, :, None, :]


def local(previous, current, field_levels, bond_levels):
    vectors, amp_count = current.shape
    site_count = field_levels.shape[0]
    devices = lax.axis_size("hi") * lax.axis_size("lo")
    local_bits = amp_count.bit_length() - 1
    global_bits = devices.bit_length() - 1
    rest_bits = local_bits - global_bits
    device = lax.axis_index("hi") * lax.axis_size("lo") + lax.axis_index("lo")
    local_index = lax.iota(jnp.int32, amp_count)
    top_width = 2**global_bits
    low_width = 2**rest_bits

    def position(site_number):
        if site_number < global_bits:
            return rest_bits + site_number
        return site_number - global_bits

    def spin_value(site_number):
        if site_number < local_bits:
            return 0.5 - (local_index >> position(site_number) & 1).astype(jnp.float32)
        return 0.5 - (device >> site_number - local_bits & 1).astype(jnp.float32)

    fields = FIELD_STEP * field_levels.astype(jnp.float32)
    couplings = COUPLING_STEP * bond_levels.astype(jnp.float32)
    diagonal = jnp.zeros((amp_count,), jnp.float32)
    for site_number in range(site_count):
        diagonal = diagonal + fields[site_number] * spin_value(site_number)
        if site_number < site_count - 1:
            diagonal = diagonal + couplings[site_number] * spin_value(site_number) * spin_value(
                site_number + 1
            )
    top_matrix = chain_matrix(
        couplings,
        global_bits,
        [(site_number, site_number) for site_number in range(global_bits - 1)],
    )
    low_matrix = chain_matrix(
        couplings,
        rest_bits,
        [
            (site_number, site_number - global_bits)
            for site_number in range(global_bits, local_bits - 1)
        ],
    )
    blocks = current.reshape(vectors, top_width, low_width)
    applied = diagonal[None, :] * current
    applied = applied + jnp.einsum(
        "vtl,tu->vul", blocks, top_matrix, precision=lax.Precision.HIGHEST
    ).reshape(vectors, amp_count)
    applied = applied + jnp.einsum(
        "vtl,lu->vtu", blocks, low_matrix, precision=lax.Precision.HIGHEST
    ).reshape(vectors, amp_count)
    joined = cross_flip(
        current.reshape(vectors, 1, 2, top_width // 2, low_width), couplings[global_bits - 1], 0
    )
    applied = applied + joined.reshape(vectors, amp_count)
    far_matrix = chain_matrix(
        couplings,
        global_bits,
        [
            (site_number, site_number - local_bits)
            for site_number in range(local_bits, site_count - 1)
        ],
    )
    shaped = current.reshape(vectors, devices, amp_count // devices)
    arrived = lax.all_to_all(shaped, ("hi", "lo"), split_axis=1, concat_axis=1, tiled=True)
    count = arrived.shape[0]
    bond_terms = jnp.einsum(
        "vtl,tu->vul", arrived, far_matrix, precision=lax.Precision.HIGHEST
    ).reshape(count, amp_count)
    seam = cross_flip(
        arrived.reshape(count, top_width // 2, 2, 1, low_width),
        couplings[local_bits - 1],
        rest_bits - 1,
    )
    bond_terms = bond_terms + seam.reshape(count, amp_count)
    remote_part = lax.all_to_all(
        bond_terms.reshape(arrived.shape), ("hi", "lo"), split_axis=1, concat_axis=1, tiled=True
    ).reshape(vectors, amp_count)
    filtered = 4.0 / site_count * (applied + remote_part) - previous
    local_gram = jnp.dot(filtered, filtered.T, precision=lax.Precision.HIGHEST) / (
        amp_count * devices
    )
    gram_matrix = lax.psum(local_gram, ("hi", "lo"))
    lower_factor = jnp.linalg.cholesky(gram_matrix)
    inverse = jax.scipy.linalg.solve_triangular(
        lower_factor, jnp.eye(vectors, dtype=jnp.float32), lower=True
    )
    ortho_block = jnp.dot(inverse, filtered, precision=lax.Precision.HIGHEST)
    return (ortho_block, lower_factor.T)


def solution(mesh):
    in_specs = (P(None, ("hi", "lo")), P(None, ("hi", "lo")), P(), P())
    out_specs = (P(None, ("hi", "lo")), P())
    return jax.shard_map(local, mesh=mesh, in_specs=in_specs, out_specs=out_specs, check_vma=False)
```

profile of v0, /device:TPU:1, one launch (start us, length us, event | category | flops | bytes accessed | tf_op | source)
XLA Modules:
  0.0 200.1 jit_solution(15617030087911046846)
XLA Ops:
  0.6 3.2 %copy_bitcast_fusion = f32[32,128,128]{2,0,1:T(8,128)} fusion(f32[32,16384]{1,0:T(8,128)} %param.5), kind=kLoop, calls=%fused_computation.6 | loop fusion | bytes 4194304 | tf_op jit(solution)/shard_map/reshape | solution.py:77
  3.8 11.5 %all-to-all-start = ((f32[32,128,128]{2,0,1:T(8,128)}), f32[32,128,128]{2,0,1:T(8,128)S(1)}, u32[]{:S(2)}, u32[]{:S(2)}) async-start(f32[32,128,128]{2,0,1:T(8,128)} %copy_bitcast_fusion), calls=%async_computation | async-start | bytes 4194304 | tf_op jit(solution)/shard_map/all_to_all | solution.py:98
  15.4 0.7 fusion.153
  20.4 25.0 %all-to-all-done = f32[32,128,128]{2,0,1:T(8,128)S(1)} async-done(((f32[32,128,128]{2,0,1:T(8,128)}), f32[32,128,128]{2,0,1:T(8,128)S(1)}, u32[]{:S(2)}, u32[]{:S(2)}) %all-to-all-start) | async-done | bytes 2097184 | tf_op jit(solution)/shard_map/all_to_all | solution.py:98
  45.4 2.3 %fusion.7 = f32[32,64,2,128]{3,1,2,0:T(8,128)S(1)} fusion(f32[32,64,2,128]{3,0,2,1:T(8,128)S(1)} %bitcast.129, s32[128]{0:T(128)S(1)} %iota_xor_fusion), kind=kOutput, calls=%fused_computation.14 | convolution fusion | flops 805322752 | bytes 4194816 | tf_op jit(solution)/shard_map/vatbl,lj->vatbj/dot_general | solution.py:26
  48.1 1.7 copy.31
  49.8 3.2 %bitcast_add_fusion.3 = f32[32,128,128]{2,1,0:T(8,128)S(1)} fusion(f32[32,128,128]{2,1,0:T(8,128)S(1)} %bitcast.133, f32[32,128,128]{2,0,1:T(8,128)S(1)} %all-to-all-done, f32[]{:T(128)S(6)} %mul.670, f32[]{:T(128)S(6)} %mul.669, f32[]{:T(128)S(6)} %mul.668, f32[]{:T(128)S(6)} %mul.667, f32[]{:T(128)S(6)} %mul.666, f32[]{:T(128)S(6)} %mul.665, ...), kind=kOutput, calls=%fused_computation.7 | convolution fusion | flops 806207488 | bytes 6295320 | tf_op jit(solution)/shard_map/vtl,tu->vul/dot_general | solution.py:100
  53.0 2.5 %copy.32 = f32[32,128,128]{2,0,1:T(8,128)} copy(f32[32,128,128]{2,1,0:T(8,128)S(1)} %bitcast_add_fusion.3) | data formatting | bytes 4194304 | tf_op jit(solution)/shard_map/add | solution.py:108
  55.5 5.9 %all-to-all-start.1 = ((f32[32,128,128]{2,0,1:T(8,128)}), f32[32,128,128]{2,0,1:T(8,128)}, u32[]{:S(2)}, u32[]{:S(2)}) async-start(f32[32,128,128]{2,0,1:T(8,128)} %copy.32), calls=%async_computation.1 | async-start | bytes 4194304 | tf_op jit(solution)/shard_map/all_to_all | solution.py:109
  61.4 0.7 fusion.151
  74.1 2.0 copy.42
  76.1 3.4 %convolution_bitcast_fusion.1 = f32[32,128,128]{1,2,0:T(8,128)} fusion(f32[32,128,128]{2,1,0:T(8,128)S(1)} %bitcast.125, f32[]{:T(128)S(6)} %mul.659, f32[]{:T(128)S(6)} %mul.658, f32[]{:T(128)S(6)} %mul.657, f32[]{:T(128)S(6)} %mul.656, f32[]{:T(128)S(6)} %mul.655, f32[]{:T(128)S(6)} %mul.654, s32[128]{0:T(128)S(1)} %get-tuple-element.52, ...), kind=kOutput, calls=%fused_computation.16 | convolution fusion | flops 805683200 | bytes 4198168 | tf_op jit(solution)/shard_map/vtl,lu->vtu/dot_general | solution.py:82
  79.5 2.9 %copy.27 = f32[32,128,128]{2,1,0:T(8,128)} copy(f32[32,128,128]{1,2,0:T(8,128)} %convolution_bitcast_fusion.1) | data formatting | bytes 4194304 | tf_op jit(solution)/shard_map/vtl,lu->vtu/dot_general | solution.py:82
  86.7 17.3 %add_add_fusion = f32[16384]{0:T(1024)S(1)} fusion(f32[]{:T(128)S(6)} %mul.645, f32[]{:T(128)S(6)} %mul.644, f32[]{:T(128)S(6)} %mul.642, f32[]{:T(128)S(6)} %mul.641, f32[]{:T(128)S(6)} %mul.639, f32[]{:T(128)S(6)} %mul.638, f32[]{:T(128)S(6)} %mul.636, f32[]{:T(128)S(6)} %mul.635, f32[]{:T(128)S(6)} %mul.633, f32[]{:T(128)S(6)} %mul.632, f32[]{:T(128)S(6)} %mul.630, ...), kind=kLoop, calls=%fused_computation.63 | loop fusion | flops 2260992 | bytes 65704 | tf_op jit(solution)/shard_map/add | solution.py:59
  104.1 1.1 convolution_bitcast_fusion
  105.2 1.6 multiply_multiply_fusion.1
  106.8 3.4 %fusion.14 = f32[128,32,128]{2,0,1:T(8,128)} fusion(f32[32,128,128]{2,1,0:T(8,128)S(1)} %bitcast.127, f32[]{:T(128)S(6)} %mul.653, s32[128]{0:T(128)S(1)} %get-tuple-element.52, f32[]{:T(128)S(6)} %mul.652, s32[128]{0:T(128)S(1)} %get-tuple-element.53, f32[]{:T(128)S(6)} %mul.651, s32[128]{0:T(128)S(1)} %get-tuple-element.54, f32[]{:T(128)S(6)} %mul.650, ...), kind=kOutput, calls=%fused_computation.20 | convolution fusion | flops 805683200 | bytes 4198168 | tf_op jit(solution)/shard_map/vtl,tu->vul/dot_general | solution.py:79
  110.2 9.6 %fusion.2 = f32[32,16384]{1,0:T(8,128)S(1)} fusion(f32[32,16384]{1,0:T(8,128)} %param.4, f32[4,8,128,128]{3,2,1,0:T(8,128)} %bitcast.130, f32[4,8,128,128]{3,2,1,0:T(8,128)} %bitcast.132, f32[4,8,128,128]{3,2,1,0:T(8,128)} %bitcast.131, f32[32,16384]{1,0:T(8,128)} %param.5, f32[16384]{0:T(1024)S(1)} %add_add_fusion, f32[32,128,128]{2,0,1:T(8,128)} %all-to-all-done.1), kind=kLoop, calls=%fused_computation.3 | loop fusion | flops 3670016 | bytes 14745600 | tf_op jit(solution)/shard_map/sub | solution.py:112
  119.8 1.8 convolution_multiply_fusion
  121.6 67.6 %psum.7 = f32[32,32]{0,1:T(8,128)S(1)} all-reduce(f32[32,32]{0,1:T(8,128)S(1)} %convolution_multiply_fusion), channel_id=1, replica_groups=mesh['hi'=16,'lo'=8] {'hi','lo'}, use_global_device_ids=true, to_apply=%region_0.1 | all-reduce | flops 1024 | bytes 8192 | tf_op jit(solution)/shard_map/psum | solution.py:116
  189.3 2.9 %cholesky.17 = f32[32,32]{1,0:T(8,128)S(1)} custom-call(f32[32,32]{1,0:T(8,128)S(1)} %fusion.138), custom_call_target="Cholesky" | custom-call | tf_op jit(solution)/shard_map/jit(cholesky)/cholesky | solution.py:117
  193.5 2.4 %custom-call.7 = f32[1,32,32]{1,2,0:T(8,128)S(1)} custom-call(f32[1,32,32]{2,1,0:T(8,128)S(1)} %get-tuple-element.11), custom_call_target="InvertDiagBlocksLowerTriangular" | custom-call | tf_op jit(solution)/shard_map/jit(_solve_triangular)/triangular_solve | solution.py:118
  196.2 3.2 %fusion.154 = f32[32,16384]{1,0:T(8,128)} fusion(f32[32,32]{1,0:T(8,128)S(1)} %fusion.136, f32[32,16384]{1,0:T(8,128)S(1)} %fusion.2), kind=kOutput, calls=%fused_computation.175 | convolution fusion | flops 201326592 | bytes 4198400 | tf_op jit(solution)/shard_map/dot_general | solution.py:121
  199.4 0.7 copy.36
  (27 shorter events, 2.6 us)
Async XLA Ops:
  3.8 11.5 %copy-start = (s32[20]{0:T(128)S(1)}, s32[20]{0:T(128)}, u32[]{:S(2)}) copy-start(s32[20]{0:T(128)} %param.7) | copy-start | bytes 244
  3.8 16.6 %copy-start.1 = (s32[21]{0:T(128)S(1)}, s32[21]{0:T(128)}, u32[]{:S(2)}) copy-start(s32[21]{0:T(128)} %param.6) | copy-start | bytes 256
  3.8 41.6 %all-to-all-start = ((f32[32,128,128]{2,0,1:T(8,128)}), f32[32,128,128]{2,0,1:T(8,128)S(1)}, u32[]{:S(2)}, u32[]{:S(2)}) async-start(f32[32,128,128]{2,0,1:T(8,128)} %copy_bitcast_fusion), calls=%async_computation | async-start | bytes 4194304 | tf_op jit(solution)/shard_map/all_to_all | solution.py:98
  55.5 54.7 %all-to-all-start.1 = ((f32[32,128,128]{2,0,1:T(8,128)}), f32[32,128,128]{2,0,1:T(8,128)}, u32[]{:S(2)}, u32[]{:S(2)}) async-start(f32[32,128,128]{2,0,1:T(8,128)} %copy.32), calls=%async_computation.1 | async-start | bytes 4194304 | tf_op jit(solution)/shard_map/all_to_all | solution.py:109
where the time goes:
time: 201 us; the launch traced here: 200 us
  blocking collectives  67.6 us (34%)
  other arithmetic  35.6 us (18%)
  waiting for transfers between devices  25 us (12%)
  between operations  20.7 us (10%)
  matrix products  18.7 us (9%)
  starting transfers between devices  17.4 us (9%)
  local copies, waits for them, and re-layouts  15.1 us (8%)
    psum x1, blocking collectives, local(): gram_matrix = lax.psum(local_gram, ('hi', 'lo'))  67.6 us
    all_to_all x1, waiting for transfers between devices, local(): lax.all_to_all(shaped, ('hi', 'lo'), split_axis=1, concat_axis=1, tiled=T...  25 us
    add x1, other arithmetic, local(): diagonal = diagonal + fields[site_number] * spin_value(site_number)  17.3 us
    all_to_all x1, starting transfers between devices, local(): lax.all_to_all(shaped, ('hi', 'lo'), split_axis=1, concat_axis=1, tiled=T...  11.5 us
    sub x1, other arithmetic, local(): filtered = 4.0 / site_count * (applied + remote_part) - previous  9.63 us
    all_to_all x1, starting transfers between devices, local(): lax.all_to_all(bond_terms.reshape(arrived.shape), ('hi', 'lo'), split_axi...  5.89 us
  transfers between devices with their start and end apart: 2, of which 1 were waited for; matrix products, arithmetic and copies ran while one was open for 17% of the time, Pallas kernels for 0%

commit v1 on v0

--- a/solution.py
+++ b/solution.py
@@ -113,7 +113,7 @@
     local_gram = jnp.dot(filtered, filtered.T, precision=lax.Precision.HIGHEST) / (
         amp_count * devices
     )
-    gram_matrix = lax.psum(local_gram, ("hi", "lo"))
+    gram_matrix = jnp.sum(lax.all_gather(local_gram, ("hi", "lo")), axis=0)
     lower_factor = jnp.linalg.cholesky(gram_matrix)
     inverse = jax.scipy.linalg.solve_triangular(
         lower_factor, jnp.eye(vectors, dtype=jnp.float32), lower=True

time: 201 us -> 177 us (0.88)
  blocking collectives: 67.6 us -> 42.1 us
    psum x1 -> x0, blocking collectives: 67.6 us -> none  [local(): gram_matrix = lax.psum(local_gram, ('hi', 'lo'))]
    all_gather x0 -> x1, blocking collectives: none -> 42.1 us  [local(): gram_matrix = jnp.sum(lax.all_gather(local_gram, ('hi', 'lo')), axis=0)]
  transfers between devices with their start and end apart: 2 -> 2, of which waited for: 1 -> 1; matrix products, arithmetic and copies ran while one was open for 17% -> 19% of each run, Pallas kernels for 0% -> 0%
where the time goes in v1:
time: 177 us; the launch traced here: 176 us
  blocking collectives  42.1 us (24%)
  other arithmetic  37.4 us (21%)
  waiting for transfers between devices  25 us (14%)
  between operations  20.7 us (12%)
  matrix products  18.7 us (11%)
  starting transfers between devices  17.4 us (10%)
  local copies, waits for them, and re-layouts  15.1 us (9%)
    all_gather x1, blocking collectives, local(): gram_matrix = jnp.sum(lax.all_gather(local_gram, ('hi', 'lo')), axis=0)  42.1 us
    all_to_all x1, waiting for transfers between devices, local(): lax.all_to_all(shaped, ('hi', 'lo'), split_axis=1, concat_axis=1, tiled=T...  25 us
    add x1, other arithmetic, local(): diagonal = diagonal + fields[site_number] * spin_value(site_number)  17.3 us
    all_to_all x1, starting transfers between devices, local(): lax.all_to_all(shaped, ('hi', 'lo'), split_axis=1, concat_axis=1, tiled=T...  11.5 us
    sub x1, other arithmetic, local(): filtered = 4.0 / site_count * (applied + remote_part) - previous  9.63 us
    all_to_all x1, starting transfers between devices, local(): lax.all_to_all(bond_terms.reshape(arrived.shape), ('hi', 'lo'), split_axi...  5.89 us
    another operation x3, other arithmetic, local(): lower_factor = jnp.linalg.cholesky(gram_matrix)  3.59 us
  transfers between devices with their start and end apart: 2, of which 1 were waited for; matrix products, arithmetic and copies ran while one was open for 19% of the time, Pallas kernels for 0%

profile of v1, /device:TPU:1, one launch (start us, length us, event | category | flops | bytes accessed | tf_op | source)
XLA Modules:
  0.0 176.4 jit_solution(8006622952608969433)
XLA Ops:
  0.6 3.2 %copy_bitcast_fusion = f32[32,128,128]{2,0,1:T(8,128)} fusion(f32[32,16384]{1,0:T(8,128)} %param.5), kind=kLoop, calls=%fused_computation.6 | loop fusion | bytes 4194304 | tf_op jit(solution)/shard_map/reshape | solution.py:77
  3.8 11.5 %all-to-all-start = ((f32[32,128,128]{2,0,1:T(8,128)}), f32[32,128,128]{2,0,1:T(8,128)S(1)}, u32[]{:S(2)}, u32[]{:S(2)}) async-start(f32[32,128,128]{2,0,1:T(8,128)} %copy_bitcast_fusion), calls=%async_computation | async-start | bytes 4194304 | tf_op jit(solution)/shard_map/all_to_all | solution.py:98
  15.4 0.7 fusion.153
  20.4 25.0 %all-to-all-done = f32[32,128,128]{2,0,1:T(8,128)S(1)} async-done(((f32[32,128,128]{2,0,1:T(8,128)}), f32[32,128,128]{2,0,1:T(8,128)S(1)}, u32[]{:S(2)}, u32[]{:S(2)}) %all-to-all-start) | async-done | bytes 2097184 | tf_op jit(solution)/shard_map/all_to_all | solution.py:98
  45.4 2.3 %fusion.7 = f32[32,64,2,128]{3,1,2,0:T(8,128)S(1)} fusion(f32[32,64,2,128]{3,0,2,1:T(8,128)S(1)} %bitcast.130, s32[128]{0:T(128)S(1)} %iota_xor_fusion), kind=kOutput, calls=%fused_computation.14 | convolution fusion | flops 805322752 | bytes 4194816 | tf_op jit(solution)/shard_map/vatbl,lj->vatbj/dot_general | solution.py:26
  48.1 1.7 copy.28
  49.8 3.2 %bitcast_add_fusion.3 = f32[32,128,128]{2,1,0:T(8,128)S(1)} fusion(f32[32,128,128]{2,1,0:T(8,128)S(1)} %bitcast.135, f32[32,128,128]{2,0,1:T(8,128)S(1)} %all-to-all-done, f32[]{:T(128)S(6)} %mul.670, f32[]{:T(128)S(6)} %mul.669, f32[]{:T(128)S(6)} %mul.668, f32[]{:T(128)S(6)} %mul.667, f32[]{:T(128)S(6)} %mul.666, f32[]{:T(128)S(6)} %mul.665, ...), kind=kOutput, calls=%fused_computation.7 | convolution fusion | flops 806207488 | bytes 6295320 | tf_op jit(solution)/shard_map/vtl,tu->vul/dot_general | solution.py:100
  53.0 2.5 %copy.29 = f32[32,128,128]{2,0,1:T(8,128)} copy(f32[32,128,128]{2,1,0:T(8,128)S(1)} %bitcast_add_fusion.3) | data formatting | bytes 4194304 | tf_op jit(solution)/shard_map/add | solution.py:108
  55.5 5.9 %all-to-all-start.1 = ((f32[32,128,128]{2,0,1:T(8,128)}), f32[32,128,128]{2,0,1:T(8,128)}, u32[]{:S(2)}, u32[]{:S(2)}) async-start(f32[32,128,128]{2,0,1:T(8,128)} %copy.29), calls=%async_computation.1 | async-start | bytes 4194304 | tf_op jit(solution)/shard_map/all_to_all | solution.py:109
  61.4 0.7 fusion.151
  74.1 2.0 %copy.37 = f32[4,8,128,128]{3,2,1,0:T(8,128)S(1)} copy(f32[4,8,128,128]{3,1,2,0:T(8,128)} %bitcast.129) | data formatting | bytes 4194304
  76.1 3.4 %convolution_bitcast_fusion.1 = f32[32,128,128]{1,2,0:T(8,128)} fusion(f32[32,128,128]{2,1,0:T(8,128)S(1)} %bitcast.126, f32[]{:T(128)S(6)} %mul.659, f32[]{:T(128)S(6)} %mul.658, f32[]{:T(128)S(6)} %mul.657, f32[]{:T(128)S(6)} %mul.656, f32[]{:T(128)S(6)} %mul.655, f32[]{:T(128)S(6)} %mul.654, s32[128]{0:T(128)S(1)} %get-tuple-element.52, ...), kind=kOutput, calls=%fused_computation.16 | convolution fusion | flops 805683200 | bytes 4198168 | tf_op jit(solution)/shard_map/vtl,lu->vtu/dot_general | solution.py:82
  79.5 2.9 %copy.24 = f32[32,128,128]{2,1,0:T(8,128)} copy(f32[32,128,128]{1,2,0:T(8,128)} %convolution_bitcast_fusion.1) | data formatting | bytes 4194304 | tf_op jit(solution)/shard_map/vtl,lu->vtu/dot_general | solution.py:82
  86.7 17.3 %add_add_fusion = f32[16384]{0:T(1024)S(1)} fusion(f32[]{:T(128)S(6)} %mul.645, f32[]{:T(128)S(6)} %mul.644, f32[]{:T(128)S(6)} %mul.642, f32[]{:T(128)S(6)} %mul.641, f32[]{:T(128)S(6)} %mul.639, f32[]{:T(128)S(6)} %mul.638, f32[]{:T(128)S(6)} %mul.636, f32[]{:T(128)S(6)} %mul.635, f32[]{:T(128)S(6)} %mul.633, f32[]{:T(128)S(6)} %mul.632, f32[]{:T(128)S(6)} %mul.630, ...), kind=kLoop, calls=%fused_computation.63 | loop fusion | flops 2260992 | bytes 65704 | tf_op jit(solution)/shard_map/add | solution.py:59
  104.1 1.1 convolution_bitcast_fusion
  105.2 1.6 multiply_multiply_fusion.1
  106.8 3.4 %fusion.14 = f32[128,32,128]{2,0,1:T(8,128)} fusion(f32[32,128,128]{2,1,0:T(8,128)S(1)} %bitcast.128, f32[]{:T(128)S(6)} %mul.653, s32[128]{0:T(128)S(1)} %get-tuple-element.52, f32[]{:T(128)S(6)} %mul.652, s32[128]{0:T(128)S(1)} %get-tuple-element.53, f32[]{:T(128)S(6)} %mul.651, s32[128]{0:T(128)S(1)} %get-tuple-element.54, f32[]{:T(128)S(6)} %mul.650, ...), kind=kOutput, calls=%fused_computation.20 | convolution fusion | flops 805683200 | bytes 4198168 | tf_op jit(solution)/shard_map/vtl,tu->vul/dot_general | solution.py:79
  110.2 9.6 %fusion.2 = f32[32,16384]{1,0:T(8,128)S(1)} fusion(f32[32,16384]{1,0:T(8,128)} %param.4, f32[4,8,128,128]{3,2,1,0:T(8,128)} %bitcast.131, f32[4,8,128,128]{3,2,1,0:T(8,128)} %bitcast.133, f32[4,8,128,128]{3,2,1,0:T(8,128)} %bitcast.132, f32[32,16384]{1,0:T(8,128)} %param.5, f32[16384]{0:T(1024)S(1)} %add_add_fusion, f32[32,128,128]{2,0,1:T(8,128)} %all-to-all-done.1), kind=kLoop, calls=%fused_computation.3 | loop fusion | flops 3670016 | bytes 14745600 | tf_op jit(solution)/shard_map/sub | solution.py:112
  119.8 1.8 %convolution_multiply_fusion = f32[32,32]{1,0:T(8,128)S(1)} fusion(f32[32,16384]{1,0:T(8,128)S(1)} %fusion.2), kind=kOutput, calls=%fused_computation.17 | convolution fusion | flops 201327616 | bytes 2101248 | tf_op jit(solution)/shard_map/dot_general | solution.py:113
  121.6 42.1 %all-gather = f32[4096,32]{1,0:T(8,128)} all-gather(f32[32,32]{1,0:T(8,128)S(1)} %convolution_multiply_fusion), channel_id=2, replica_groups=mesh['hi'=16,'lo'=8] {'hi','lo'}, dimensions={0}, use_global_device_ids=true | all-gather | bytes 528384 | tf_op jit(solution)/shard_map/all_gather | solution.py:116
  163.7 1.8 %reduce_sum.9 = f32[32,32]{1,0:T(8,128)S(1)} reduce(f32[128,32,32]{2,1,0:T(8,128)} %bitcast.134, f32[]{:T(128)} %constant.106.clone.1), dimensions={0}, to_apply=%region_0.1 | reduce | flops 130048 | bytes 528388 | tf_op jit(solution)/shard_map/reduce_sum | solution.py:116
  165.5 2.9 %cholesky.17 = f32[32,32]{1,0:T(8,128)S(1)} custom-call(f32[32,32]{1,0:T(8,128)S(1)} %fusion.138), custom_call_target="Cholesky" | custom-call | tf_op jit(solution)/shard_map/jit(cholesky)/cholesky | solution.py:117
  169.8 2.4 %custom-call.7 = f32[1,32,32]{1,2,0:T(8,128)S(1)} custom-call(f32[1,32,32]{2,1,0:T(8,128)S(1)} %get-tuple-element.11), custom_call_target="InvertDiagBlocksLowerTriangular" | custom-call | tf_op jit(solution)/shard_map/jit(_solve_triangular)/triangular_solve | solution.py:118
  172.5 3.2 %fusion.154 = f32[32,16384]{1,0:T(8,128)} fusion(f32[32,32]{1,0:T(8,128)S(1)} %fusion.136, f32[32,16384]{1,0:T(8,128)S(1)} %fusion.2), kind=kOutput, calls=%fused_computation.175 | convolution fusion | flops 201326592 | bytes 4198400 | tf_op jit(solution)/shard_map/dot_general | solution.py:121
  (28 shorter events, 3.3 us)
Async XLA Ops:
  3.8 11.5 %copy-start = (s32[20]{0:T(128)S(1)}, s32[20]{0:T(128)}, u32[]{:S(2)}) copy-start(s32[20]{0:T(128)} %param.7) | copy-start | bytes 244
  3.8 16.6 %copy-start.1 = (s32[21]{0:T(128)S(1)}, s32[21]{0:T(128)}, u32[]{:S(2)}) copy-start(s32[21]{0:T(128)} %param.6) | copy-start | bytes 256
  3.8 41.6 %all-to-all-start = ((f32[32,128,128]{2,0,1:T(8,128)}), f32[32,128,128]{2,0,1:T(8,128)S(1)}, u32[]{:S(2)}, u32[]{:S(2)}) async-start(f32[32,128,128]{2,0,1:T(8,128)} %copy_bitcast_fusion), calls=%async_computation | async-start | bytes 4194304 | tf_op jit(solution)/shard_map/all_to_all | solution.py:98
  55.5 54.7 %all-to-all-start.1 = ((f32[32,128,128]{2,0,1:T(8,128)}), f32[32,128,128]{2,0,1:T(8,128)}, u32[]{:S(2)}, u32[]{:S(2)}) async-start(f32[32,128,128]{2,0,1:T(8,128)} %copy.29), calls=%async_computation.1 | async-start | bytes 4194304 | tf_op jit(solution)/shard_map/all_to_all | solution.py:109
